TPU v7x, 128 devices: a whole 4x4x4 slice. The times are simulated.
128 devices in a mesh: freq: 16 (over x, y), slab: 8 (over z, core).
Axes of the slice: x: 4, y: 4, z: 4, core: 2. Of those that a mesh axis runs over, the one named last changes fastest.
Arguments:
- fine_model: bfloat16 [2048, 2048], P(('freq', 'slab')), may hold values from 0.5 to 2
- resample: bfloat16 [16, 1024, 2048], P('freq', 'slab'), may hold values from -0.125 to 0.125
- lateral: bfloat16 [2048, 2048], replicated, may hold values from -0.0625 to 0.0625
- shift: float32 [16], P('freq'), may hold values from 0.5 to 4
- source: float32 [16, 1024, 2048], P('freq', 'slab'), may hold values from -6 to 6
- receiver: float32 [16, 1024, 2048], P('freq', 'slab'), may hold values from -6 to 6
Outputs:
- image: float32 [2048, 2048], P(('freq', 'slab'))
All inputs are finite; a program needn't handle non-finite values.
Results may differ from a plain program's by a relative error of at most 0.0029.
Values may be sent and summed in bfloat16 or wider, within the bound.
A program may use at most 128 MiB of HBM per device.

v0:
```python
import jax
import jax.numpy as jnp
from jax import lax
from jax.sharding import PartitionSpec as P

SWEEPS = 8


def with_halo(value, sides, width):
    for axis, dim in sides:
        size, length = (lax.axis_size(axis), value.shape[dim])
        up = [(i, (i + 1) % size) for i in range(size - 1)]
        down = [(j, i) for i, j in up]
        last = lax.slice_in_dim(value, length - width, length, axis=dim)
        initial = lax.slice_in_dim(value, 0, width, axis=dim)
        before = lax.ppermute(last, axis, up)
        after = lax.ppermute(initial, axis, down)
        value = jnp.concatenate([before, value, after], axis=dim)
    return value


def shards(fine_model, resample, lateral, shift, source, receiver):
    oper = resample[0]
    columns = oper
    coarse = jnp.dot(
        columns,
        lax.all_gather(fine_model, ("freq", "slab"), axis=0, tiled=True),
        preferred_element_type=jnp.float32,
    )
    diag = 4.0 + shift[0] * coarse * coarse
    src = source[0]
    field = jnp.zeros(src.shape, jnp.float32)
    for sweep in range(SWEEPS):
        padded = with_halo(field, (("slab", 0),), 1)
        beside = padded[2:] + padded[:-2]
        side = jnp.dot(field.astype(jnp.bfloat16), lateral, preferred_element_type=jnp.float32)
        field = (src + 0.5 * beside + side) / diag
    partial_img = (field * receiver[0]).astype(jnp.bfloat16)
    columns = oper
    return lax.psum_scatter(
        lax.dot_general(
            columns, partial_img, (((0,), (0,)), ((), ())), preferred_element_type=jnp.float32
        ),
        ("freq", "slab"),
        scatter_dimension=0,
        tiled=True,
    )


def solution(mesh):
    in_specs = (
        P(("freq", "slab"), None),
        P("freq", "slab", None),
        P(),
        P("freq"),
        P("freq", "slab", None),
        P("freq", "slab", None),
    )
    out_specs = P(("freq", "slab"), None)
    return jax.shard_map(shards, mesh=mesh, in_specs=in_specs, out_specs=out_specs, check_vma=False)
```

profile of v0, /device:TPU:0, one launch (start us, length us, event | category | flops | bytes accessed | tf_op | source)
XLA Modules:
  0.0 849.0 jit_solution(14113085635344979376)
XLA Ops:
  6.5 0.0 copy-start
  6.5 0.0 copy-start.1
  6.5 0.0 all-gather.2.cloned.1.call-start
  6.5 0.7 all-gather.2.cloned.1.call-update
  7.3 0.0 reduce-scatter.4.cloned.1.call-start
  7.3 1.3 collective-permute-start.1
  8.6 1.3 collective-permute-start
  10.6 72.4 %all-gather.2.cloned.1.call-done = bf16[2048,2048]{1,0:T(8,128)(2,1)} async-done(((bf16[16,2048]{1,0:T(8,128)(2,1)}), bf16[2048,2048]{1,0:T(8,128)(2,1)}) %all-gather.2.cloned.1.call-update) | async-done | bytes 8388624 | tf_op jit(solution)/shard_map/all_gather | solution.py:27
  83.0 0.0 slice-start
  83.0 0.0 copy-done
  83.0 0.0 slice-start.1
  83.0 4.8 fusion.5
  87.8 0.0 collective-permute-done.1
  87.8 0.0 collective-permute-done
  87.8 0.0 copy-done.1
  87.8 0.0 slice-done
  87.8 1.0 slice-done.1
  88.8 1.3 fusion.4
  90.2 1.3 collective-permute-start.2
  91.5 3.0 collective-permute-start.3
  94.5 0.0 collective-permute-done.2
  94.5 0.8 collective-permute-done.3
  95.3 1.6 fusion.41
  97.0 1.3 collective-permute-start.4
  98.3 4.0 collective-permute-start.5
  102.3 0.0 collective-permute-done.4
  102.3 0.8 collective-permute-done.5
  103.1 1.6 fusion.36
  104.7 1.3 collective-permute-start.6
  106.0 4.8 collective-permute-start.7
  110.8 0.0 collective-permute-done.6
  110.8 0.8 collective-permute-done.7
  111.6 1.6 fusion.31
  113.2 1.3 collective-permute-start.8
  114.5 4.8 collective-permute-start.9
  119.3 0.0 collective-permute-done.8
  119.3 0.8 collective-permute-done.9
  120.1 1.6 fusion.26
  121.8 1.3 collective-permute-start.10
  123.1 0.0 copy-start.2
  123.1 4.9 collective-permute-start.11
  128.0 0.0 collective-permute-done.10
  128.0 0.8 collective-permute-done.11
  128.8 1.6 fusion.21
  130.4 1.3 collective-permute-start.12
  131.7 5.0 collective-permute-start.13
  136.7 0.0 collective-permute-done.12
  136.7 0.6 collective-permute-done.13
  137.3 0.0 copy-done.2
  137.3 1.6 fusion.16
  139.0 1.3 collective-permute-start.14
  140.3 4.8 collective-permute-start.15
  145.0 0.0 collective-permute-done.14
  145.1 0.8 collective-permute-done.15
  145.9 12.7 %convolution_bitcast_fusion = f32[2048,2048]{0,1:T(8,128)} fusion(f32[1,128,2048]{2,1,0:T(8,128)} %param.11, f32[128,2048]{1,0:T(8,128)S(1)} %fusion.5, f32[128,2048]{1,0:T(8,128)S(1)} %fusion.16, f32[1,2048]{1,0:T(1,128)S(1)} %collective-permute-done.15, f32[1,2048]{1,0:T(1,128)S(1)} %collective-permute-done.14, f32[1,128,2048]{2,1,0:T(8,128)} %param.10, ...), kind=kOutput, calls=%fused_computation | convolution fusion | flops 2150105088 | bytes 29900800 | tf_op jit(solution)/shard_map/dot_general | solution.py:41
  158.5 17.6 %copy.9 = f32[2048,2048]{1,0:T(8,128)} copy(f32[2048,2048]{0,1:T(8,128)} %convolution_bitcast_fusion) | data formatting | bytes 33554432
  176.1 0.0 reduce-scatter.4.cloned.1.call-update
  176.1 666.1 %reduce-scatter.4.cloned.1.call-done = f32[16,2048]{1,0:T(8,128)} async-done(((f32[2048,2048]{1,0:T(8,128)}), f32[16,2048]{1,0:T(8,128)}) %reduce-scatter.4.cloned.1.call-update) | async-done | bytes 131088 | tf_op jit(solution)/shard_map/reduce_scatter | solution.py:40
  (9 shorter events, 0.1 us)
Async XLA Ops:
  6.5 76.4 %copy-start = (bf16[1,128,2048]{2,1,0:T(8,128)(2,1)S(1)}, bf16[1,128,2048]{2,1,0:T(8,128)(2,1)}, u32[]{:S(2)}) copy-start(bf16[1,128,2048]{2,1,0:T(8,128)(2,1)} %param.7) | copy-start | bytes 1572868
  6.5 81.3 %copy-start.1 = (f32[1,128,2048]{2,1,0:T(8,128)S(1)}, f32[1,128,2048]{2,1,0:T(8,128)}, u32[]{:S(2)}) copy-start(f32[1,128,2048]{2,1,0:T(8,128)} %param.10) | copy-start | bytes 3145732
  6.5 76.4 %all-gather.2.cloned.1.call-start = ((), (), s32[]{:S(2)}) async-start(), calls=%async_computation.1 | async-start | bytes 8454144 | tf_op jit(solution)/shard_map/all_gather | solution.py:27
  7.3 834.9 %reduce-scatter.4.cloned.1.call-start = ((), (), s32[]{:S(2)}) async-start(), calls=%async_computation.2 | async-start | bytes 16908288 | tf_op jit(solution)/shard_map/reduce_scatter | solution.py:40
  7.3 80.5 %collective-permute-start.1 = (f32[1,2048]{1,0:T(1,128)S(1)}, f32[1,2048]{1,0:T(1,128)S(1)}, u32[]{:S(2)}, u32[]{:S(2)}) collective-permute-start(f32[1,2048]{1,0:T(1,128)S(1)} %broadcast.12), channel_id=1, source_target_pairs={{0,1},{1,2},{2,3},{3,4},{4,5},{5,6},{6,7},{8,9},{9,10},{10,11},{11... | collective-permute-start | bytes 24584 | tf_op jit(solution)/shard_map/ppermute | solution.py:16
  8.6 79.2 %collective-permute-start = (f32[1,2048]{1,0:T(1,128)S(1)}, f32[1,2048]{1,0:T(1,128)S(1)}, u32[]{:S(2)}, u32[]{:S(2)}) collective-permute-start(f32[1,2048]{1,0:T(1,128)S(1)} %broadcast.12), channel_id=1, source_target_pairs={{1,0},{2,1},{3,2},{4,3},{5,4},{6,5},{7,6},{9,8},{10,9},{11,10},{12... | collective-permute-start | bytes 24584 | tf_op jit(solution)/shard_map/ppermute | solution.py:17
  83.0 4.9 slice-start
  83.0 5.8 slice-start.1
  90.2 4.3 collective-permute-start.2
  91.5 3.8 collective-permute-start.3
  97.0 5.3 collective-permute-start.4
  98.3 4.8 collective-permute-start.5
  104.7 6.1 collective-permute-start.6
  106.0 5.6 collective-permute-start.7
  113.2 6.1 collective-permute-start.8
  114.5 5.6 collective-permute-start.9
  121.8 6.2 collective-permute-start.10
  123.1 14.3 %copy-start.2 = (f32[1,128,2048]{2,1,0:T(8,128)S(1)}, f32[1,128,2048]{2,1,0:T(8,128)}, u32[]{:S(2)}) copy-start(f32[1,128,2048]{2,1,0:T(8,128)} %param.10) | copy-start | bytes 3145732
  123.1 5.7 collective-permute-start.11
  130.4 6.3 collective-permute-start.12
  131.7 5.6 collective-permute-start.13
  139.0 6.1 collective-permute-start.14
  140.3 5.6 collective-permute-start.15
Sparse Core Ops, SparseCore 0:
  10.3 72.5 all-gather.1
  176.3 665.9 reduce-scatter.3
where the time goes:
time: 850 us; the launch traced here: 849 us
  waiting for transfers between devices  745 us (88%)
  starting transfers between devices  42.9 us (5%)
  matrix products  28.4 us (3%)
  local copies, waits for them, and re-layouts  18.7 us (2%)
  between operations  14.4 us (2%)
    reduce_scatter x1, waiting for transfers between devices, shards(): lax.psum_scatter(lax.dot_general(columns, partial_img, (((0,), (0,)), (()...  666 us
    all_gather x1, waiting for transfers between devices, shards(): lax.all_gather(fine_model, ('freq', 'slab'), axis=0, tiled=True)  72.4 us
    ppermute x8, starting transfers between devices, with_halo(): before = lax.ppermute(last, axis, up)  32.5 us
    unnamed x11, local copies, waits for them, and re-layouts  18.6 us
  transfers between devices with their start and end apart: 18, of which 9 were waited for; matrix products, arithmetic and copies ran while one was open for 1% of the time, Pallas kernels for 0%

commit v1 on v0

--- a/solution.py
+++ b/solution.py
@@ -4,6 +4,18 @@
 from jax.sharding import PartitionSpec as P
 
 SWEEPS = 8
+
+
+def settle_array(s0):
+    return jnp.concatenate(
+        jax.lax.all_to_all(
+            jnp.stack([s0] * jax.lax.axis_size(("freq", "slab"))),
+            concat_axis=0,
+            split_axis=0,
+            axis_name=("freq", "slab"),
+        ),
+        0,
+    )
 
 
 def with_halo(value, sides, width):
@@ -22,11 +34,7 @@
 def shards(fine_model, resample, lateral, shift, source, receiver):
     oper = resample[0]
     columns = oper
-    coarse = jnp.dot(
-        columns,
-        lax.all_gather(fine_model, ("freq", "slab"), axis=0, tiled=True),
-        preferred_element_type=jnp.float32,
-    )
+    coarse = jnp.dot(columns, settle_array(fine_model), preferred_element_type=jnp.float32)
     diag = 4.0 + shift[0] * coarse * coarse
     src = source[0]
     field = jnp.zeros(src.shape, jnp.float32)

time: 850 us -> 901 us (1.060)
  waiting for transfers between devices: 745 us -> 775 us
  starting transfers between devices: 42.9 us -> 55.5 us
    all_to_all x0 -> x1, waiting for transfers between devices: none -> 98.9 us  [settle_array(): jax.lax.all_to_all(jnp.stack([s0] * jax.lax.axis_size(('freq', 'slab'))),...]
    all_gather x1 -> x0, waiting for transfers between devices: 72.4 us -> none  [shards(): lax.all_gather(fine_model, ('freq', 'slab'), axis=0, tiled=True)]
    all_to_all x0 -> x1, starting transfers between devices: none -> 11.7 us  [settle_array(): jax.lax.all_to_all(jnp.stack([s0] * jax.lax.axis_size(('freq', 'slab'))),...]
where the time goes in v1:
time: 901 us; the launch traced here: 900 us
  waiting for transfers between devices  775 us (86%)
  starting transfers between devices  55.5 us (6%)
  matrix products  32.1 us (4%)
  local copies, waits for them, and re-layouts  23 us (3%)
  between operations  14.4 us (2%)
    reduce_scatter x1, waiting for transfers between devices, shards(): lax.psum_scatter(lax.dot_general(columns, partial_img, (((0,), (0,)), (()...  671 us
    all_to_all x1, waiting for transfers between devices, settle_array(): jax.lax.all_to_all(jnp.stack([s0] * jax.lax.axis_size(('freq', 'slab'))),...  98.9 us
    ppermute x8, starting transfers between devices, with_halo(): before = lax.ppermute(last, axis, up)  33.5 us
  transfers between devices with their start and end apart: 18, of which 9 were waited for; matrix products, arithmetic and copies ran while one was open for 1% of the time, Pallas kernels for 0%

profile of v1, /device:TPU:0, one launch (start us, length us, event | category | flops | bytes accessed | tf_op | source)
XLA Modules:
  0.0 900.2 jit_solution(5276830409550822209)
XLA Ops:
  6.5 0.0 copy-start
  6.5 5.2 stack.2
  11.7 11.7 %all-to-all-start = ((bf16[128,16,2048]{2,1,0:T(8,128)(2,1)}), bf16[128,16,2048]{2,1,0:T(8,128)(2,1)}, u32[]{:S(2)}, u32[]{:S(2)}) async-start(bf16[128,16,2048]{2,1,0:T(8,128)(2,1)} %stack.2), calls=%async_computation | async-start | bytes 16777216 | tf_op jit(solution)/shard_map/all_to_all | solution.py:11
  23.4 0.0 copy-start.1
  23.4 0.0 reduce-scatter.4.cloned.1.call-start
  23.5 1.4 collective-permute-start.1
  24.9 1.3 collective-permute-start
  26.9 98.9 %all-to-all-done = bf16[128,16,2048]{2,1,0:T(8,128)(2,1)} async-done(((bf16[128,16,2048]{2,1,0:T(8,128)(2,1)}), bf16[128,16,2048]{2,1,0:T(8,128)(2,1)}, u32[]{:S(2)}, u32[]{:S(2)}) %all-to-all-start) | async-done | bytes 8388640 | tf_op jit(solution)/shard_map/all_to_all | solution.py:11
  125.8 0.0 copy-done
  125.8 0.0 slice-start
  125.8 4.8 fusion.5
  130.6 0.0 slice-start.1
  130.6 0.0 collective-permute-done.1
  130.6 0.0 collective-permute-done
  130.6 0.0 copy-done.1
  130.6 4.9 fusion.4
  135.5 1.3 collective-permute-start.2
  136.8 3.0 collective-permute-start.3
  139.9 0.0 collective-permute-done.2
  139.9 0.8 collective-permute-done.3
  140.7 0.0 slice-done
  140.7 0.0 slice-done.1
  140.7 1.6 fusion.41
  142.3 1.3 collective-permute-start.4
  143.6 4.8 collective-permute-start.5
  148.4 0.0 collective-permute-done.4
  148.5 0.8 collective-permute-done.5
  149.3 1.6 fusion.36
  150.9 1.3 collective-permute-start.6
  152.2 4.8 collective-permute-start.7
  157.0 0.0 collective-permute-done.6
  157.0 0.8 collective-permute-done.7
  157.8 1.6 fusion.31
  159.4 1.3 collective-permute-start.8
  160.7 4.8 collective-permute-start.9
  165.5 0.0 collective-permute-done.8
  165.5 0.8 collective-permute-done.9
  166.3 1.6 fusion.26
  168.0 1.3 collective-permute-start.10
  169.3 0.0 copy-start.2
  169.3 5.1 collective-permute-start.11
  174.4 0.0 collective-permute-done.10
  174.4 0.6 collective-permute-done.11
  175.0 1.6 fusion.21
  176.6 1.3 collective-permute-start.12
  177.9 4.8 collective-permute-start.13
  182.7 0.0 collective-permute-done.12
  182.7 0.8 collective-permute-done.13
  183.5 0.0 copy-done.2
  183.5 1.6 fusion.16
  185.2 1.3 collective-permute-start.14
  186.5 4.8 collective-permute-start.15
  191.2 0.0 collective-permute-done.14
  191.3 0.8 collective-permute-done.15
  192.1 12.8 %convolution_bitcast_fusion = f32[2048,2048]{0,1:T(8,128)} fusion(f32[1,128,2048]{2,1,0:T(8,128)} %param.11, f32[128,2048]{1,0:T(8,128)S(1)} %fusion.5, f32[128,2048]{1,0:T(8,128)S(1)} %fusion.16, f32[1,2048]{1,0:T(1,128)S(1)} %collective-permute-done.15, f32[1,2048]{1,0:T(1,128)S(1)} %collective-permute-done.14, f32[1,128,2048]{2,1,0:T(8,128)} %param.10, ...), kind=kOutput, calls=%fused_computation | convolution fusion | flops 2150105088 | bytes 29900800 | tf_op jit(solution)/shard_map/dot_general | solution.py:49
  204.9 17.6 %copy.9 = f32[2048,2048]{1,0:T(8,128)} copy(f32[2048,2048]{0,1:T(8,128)} %convolution_bitcast_fusion) | data formatting | bytes 33554432
  222.5 0.0 reduce-scatter.4.cloned.1.call-update
  222.5 670.8 %reduce-scatter.4.cloned.1.call-done = f32[16,2048]{1,0:T(8,128)} async-done(((f32[2048,2048]{1,0:T(8,128)}), f32[16,2048]{1,0:T(8,128)}) %reduce-scatter.4.cloned.1.call-update) | async-done | bytes 131088 | tf_op jit(solution)/shard_map/reduce_scatter | solution.py:48
  (9 shorter events, 0.1 us)
Async XLA Ops:
  6.5 119.2 %copy-start = (bf16[1,128,2048]{2,1,0:T(8,128)(2,1)S(1)}, bf16[1,128,2048]{2,1,0:T(8,128)(2,1)}, u32[]{:S(2)}) copy-start(bf16[1,128,2048]{2,1,0:T(8,128)(2,1)} %param.7) | copy-start | bytes 1572868
  11.7 114.0 %all-to-all-start = ((bf16[128,16,2048]{2,1,0:T(8,128)(2,1)}), bf16[128,16,2048]{2,1,0:T(8,128)(2,1)}, u32[]{:S(2)}, u32[]{:S(2)}) async-start(bf16[128,16,2048]{2,1,0:T(8,128)(2,1)} %stack.2), calls=%async_computation | async-start | bytes 16777216 | tf_op jit(solution)/shard_map/all_to_all | solution.py:11
  23.4 107.2 %copy-start.1 = (f32[1,128,2048]{2,1,0:T(8,128)S(1)}, f32[1,128,2048]{2,1,0:T(8,128)}, u32[]{:S(2)}) copy-start(f32[1,128,2048]{2,1,0:T(8,128)} %param.10) | copy-start | bytes 3145732
  23.4 869.9 %reduce-scatter.4.cloned.1.call-start = ((), (), s32[]{:S(2)}) async-start(), calls=%async_computation.2 | async-start | bytes 16908288 | tf_op jit(solution)/shard_map/reduce_scatter | solution.py:48
  23.5 107.1 %collective-permute-start.1 = (f32[1,2048]{1,0:T(1,128)S(1)}, f32[1,2048]{1,0:T(1,128)S(1)}, u32[]{:S(2)}, u32[]{:S(2)}) collective-permute-start(f32[1,2048]{1,0:T(1,128)S(1)} %broadcast.14), channel_id=1, source_target_pairs={{0,1},{1,2},{2,3},{3,4},{4,5},{5,6},{6,7},{8,9},{9,10},{10,11},{11... | collective-permute-start | bytes 24584 | tf_op jit(solution)/shard_map/ppermute | solution.py:28
  24.9 105.7 %collective-permute-start = (f32[1,2048]{1,0:T(1,128)S(1)}, f32[1,2048]{1,0:T(1,128)S(1)}, u32[]{:S(2)}, u32[]{:S(2)}) collective-permute-start(f32[1,2048]{1,0:T(1,128)S(1)} %broadcast.14), channel_id=1, source_target_pairs={{1,0},{2,1},{3,2},{4,3},{5,4},{6,5},{7,6},{9,8},{10,9},{11,10},{12... | collective-permute-start | bytes 24584 | tf_op jit(solution)/shard_map/ppermute | solution.py:29
  125.8 14.9 %slice-start = ((s8[8388608]{0:T(1024)(128)(4,1)}), s8[4194304]{0:T(1024)(128)(4,1)S(1)}, s32[]{:S(2)}) async-start(s8[8388608]{0:T(1024)(128)(4,1)} %bitcast.39), calls=%async_computation.3 | async-start | bytes 8388608
  130.6 10.1 %slice-start.1 = ((s8[8388608]{0:T(1024)(128)(4,1)}), s8[4194304]{0:T(1024)(128)(4,1)S(1)}, s32[]{:S(2)}) async-start(s8[8388608]{0:T(1024)(128)(4,1)} %bitcast.39), calls=%async_computation.4 | async-start | bytes 8388608
  135.5 4.3 collective-permute-start.2
  136.8 3.8 collective-permute-start.3
  142.3 6.1 collective-permute-start.4
  143.6 5.6 collective-permute-start.5
  150.9 6.1 collective-permute-start.6
  152.2 5.6 collective-permute-start.7
  159.4 6.1 collective-permute-start.8
  160.7 5.6 collective-permute-start.9
  168.0 6.4 collective-permute-start.10
  169.3 14.3 %copy-start.2 = (f32[1,128,2048]{2,1,0:T(8,128)S(1)}, f32[1,128,2048]{2,1,0:T(8,128)}, u32[]{:S(2)}) copy-start(f32[1,128,2048]{2,1,0:T(8,128)} %param.10) | copy-start | bytes 3145732
  169.3 5.7 collective-permute-start.11
  176.6 6.1 collective-permute-start.12
  177.9 5.6 collective-permute-start.13
  185.2 6.1 collective-permute-start.14
  186.5 5.6 collective-permute-start.15
Sparse Core Ops, SparseCore 0:
  222.6 670.6 reduce-scatter.3
